TPU v7x, 32 devices: a whole 2x2x4 slice. The times are simulated.
32 devices in a mesh: ctx: 16 (over z, y, x), tp: 2 (over core).
Axes of the slice: x: 2, y: 2, z: 4, core: 2. Of those that a mesh axis runs over, the one named last changes fastest.
Arguments:
- tokens: bfloat16 [4096, 2688], P(('ctx', 'tp')), may hold values from -6 to 6
- result_grad: bfloat16 [4096, 2688], P(('ctx', 'tp')), may hold values from -6 to 6
- query_weight: bfloat16 [2688, 512], P(None, 'tp'), may hold values from -0.125 to 0.125
- key_weight: bfloat16 [2688, 256], P(None, 'tp'), may hold values from -0.125 to 0.125
- value_weight: bfloat16 [2688, 256], P(None, 'tp'), may hold values from -0.125 to 0.125
- output_weight: bfloat16 [512, 2688], P('tp'), may hold values from -0.5 to 0.5
- query_gain: float32 [128], replicated, may hold values from 0.5 to 1.5
- key_gain: float32 [128], replicated, may hold values from 0.5 to 1.5
Outputs:
- layer_output: bfloat16 [4096, 2688], P(('ctx', 'tp'))
- tokens_grad: bfloat16 [4096, 2688], P(('ctx', 'tp'))
All inputs are finite; a program needn't handle non-finite values.
Results may differ from a plain program's by a relative error of at most 0.012.
Values may be sent and summed in bfloat16 or wider, within the bound.
A program may use at most 64 MiB of HBM per device.

v0:
```python
import jax
import jax.numpy as jnp
from jax import lax
from jax.sharding import PartitionSpec as P

WINDOW = 1024


norm_epsilon = 1e-06
score_scale = 168.0 ** (-0.5)
rope_theta = 10000.0


def from_behind(block, axis, distance):
    devices = range(lax.axis_size(axis))
    route = [(i - distance, i) for i in devices if i - distance in devices]
    return lax.ppermute(block, axis, route)


def rope_tables(positions, head_size):
    half_size = head_size // 2
    exponent = jnp.arange(half_size, dtype=jnp.float32) * (2.0 / head_size)
    frequency = jnp.power(jnp.float32(rope_theta), -exponent)
    angles = positions.astype(jnp.float32)[:, None] * frequency[None, :]
    return (jnp.cos(angles), jnp.sin(angles))


def norm_rope(raw_proj, scale_gain, cosines, sines):
    row_count = raw_proj.shape[0]
    head_size = scale_gain.shape[0]
    split_heads = raw_proj.reshape(row_count, -1, head_size)
    mean_square = jnp.mean(split_heads * split_heads, axis=-1, keepdims=True)
    normed = split_heads * lax.rsqrt(mean_square + norm_epsilon) * scale_gain
    half_size = head_size // 2
    low_half = normed[..., :half_size]
    high_half = normed[..., half_size:]
    cosine_b = cosines[:, None, :]
    sine_b = sines[:, None, :]
    return jnp.concatenate(
        [low_half * cosine_b - high_half * sine_b, high_half * cosine_b + low_half * sine_b],
        axis=-1,
    )


def attend(queries, keys_all, values_all, out_grad, query_first, key_first):
    query_count = queries.shape[0]
    key_count = keys_all.shape[0]
    scores = (
        jnp.einsum("qkgh,ckh->kgqc", queries, keys_all, preferred_element_type=jnp.float32)
        * score_scale
    )
    query_pos = query_first + jnp.arange(query_count, dtype=jnp.int32)
    key_pos = key_first + jnp.arange(key_count, dtype=jnp.int32)
    distance = query_pos[:, None] - key_pos[None, :]
    allowed = (distance >= 0) & (distance < WINDOW) & (key_pos[None, :] >= 0)
    weights_raw = jnp.where(allowed, jnp.exp(scores), jnp.float32(0.0))
    denominator = jnp.sum(weights_raw, axis=-1, keepdims=True)
    weights_soft = weights_raw / denominator
    weights_low = weights_soft.astype(jnp.bfloat16)
    attended_wide = jnp.einsum(
        "kgqc,ckh->qkgh", weights_low, values_all, preferred_element_type=jnp.float32
    )
    attended = lax.optimization_barrier(attended_wide.astype(jnp.bfloat16))
    row_dots = jnp.sum(out_grad.astype(jnp.float32) * attended.astype(jnp.float32), axis=-1)
    prob_grad = jnp.einsum(
        "qkgh,ckh->kgqc", out_grad, values_all, preferred_element_type=jnp.float32
    )
    centered = prob_grad - jnp.transpose(row_dots, (1, 2, 0))[..., None]
    score_grad = (weights_soft * centered * score_scale).astype(jnp.bfloat16)
    query_grad = jnp.einsum(
        "kgqc,ckh->qkgh", score_grad, keys_all, preferred_element_type=jnp.float32
    )
    key_grad = jnp.einsum("kgqc,qkgh->ckh", score_grad, queries, preferred_element_type=jnp.float32)
    value_grad = jnp.einsum(
        "kgqc,qkgh->ckh", weights_low, out_grad, preferred_element_type=jnp.float32
    )
    return (attended, query_grad, key_grad, value_grad)


def on_device(
    tokens, result_grad, query_weight, key_weight, value_weight, output_weight, query_gain, key_gain
):
    local_rows = tokens.shape[0]
    row_count = local_rows * lax.axis_size("tp")
    head_size = query_gain.shape[0]
    query_cols = query_weight.shape[1]
    kv_cols = key_weight.shape[1]
    kv_count = kv_cols // head_size
    per_kv = query_cols // kv_cols
    stacked = jnp.stack([tokens, result_grad])
    portion = lax.all_gather(stacked, "tp", axis=1, tiled=True)
    inputs_part = portion[0]
    gradients_part = portion[1]
    query_rows = jnp.dot(inputs_part, query_weight, preferred_element_type=jnp.float32)
    key_rows = jnp.dot(inputs_part, key_weight, preferred_element_type=jnp.float32)
    value_rows = jnp.dot(inputs_part, value_weight, preferred_element_type=jnp.float32)
    grad_rows = jnp.einsum(
        "nd,hd->nh", gradients_part, output_weight, preferred_element_type=jnp.float32
    )
    joined = jnp.concatenate([query_rows, key_rows, value_rows, grad_rows], axis=1)
    query_raw = joined[:, :query_cols]
    key_raw = joined[:, query_cols : query_cols + kv_cols]
    value_raw = joined[:, query_cols + kv_cols : query_cols + 2 * kv_cols]
    out_grad = (
        joined[:, query_cols + 2 * kv_cols :]
        .astype(jnp.bfloat16)
        .reshape(row_count, kv_count, per_kv, head_size)
    )
    row_first = lax.axis_index("ctx") * row_count
    positions = row_first + jnp.arange(row_count, dtype=jnp.int32)
    cosines, sines = rope_tables(positions, head_size)
    queries = (
        norm_rope(query_raw, query_gain, cosines, sines)
        .astype(jnp.bfloat16)
        .reshape(row_count, kv_count, per_kv, head_size)
    )
    keys_own = norm_rope(key_raw, key_gain, cosines, sines).astype(jnp.bfloat16)
    values_own = value_raw.astype(jnp.bfloat16).reshape(row_count, kv_count, head_size)
    tail_rows = min(row_count, WINDOW)
    reach = WINDOW // tail_rows
    own_tail = jnp.stack([keys_own, values_own])
    arrivals = []
    message = own_tail
    for stride in range(1, reach + 1):
        sender = own_tail
        distance = stride
        message = from_behind(sender, "ctx", distance)
        arrivals.append(message)
    halo_rows = jnp.concatenate(arrivals[::-1], axis=1)
    keys_all = jnp.concatenate([halo_rows[0], keys_own], axis=0)
    values_all = jnp.concatenate([halo_rows[1], values_own], axis=0)
    attended, query_grad, key_grad, value_grad = attend(
        queries, keys_all, values_all, out_grad, row_first, row_first - WINDOW
    )
    attended_flat = attended.reshape(row_count, query_cols)
    halo_grad = jnp.stack([key_grad[:WINDOW], value_grad[:WINDOW]])
    returned = jnp.zeros((2, tail_rows, kv_count, head_size), jnp.float32)
    for turn_index in range(reach):
        portion_stride = turn_index + 1
        sender = halo_grad[
            :, WINDOW - portion_stride * tail_rows : WINDOW - (portion_stride - 1) * tail_rows
        ]
        distance = -(turn_index + 1)
        arrived = from_behind(sender.astype(jnp.bfloat16), "ctx", distance).astype(sender.dtype)
        returned = returned + arrived
    keep_rows = row_count - tail_rows
    key_grad_own = key_grad[WINDOW:]
    value_grad_own = value_grad[WINDOW:]
    key_grad_own = jnp.concatenate([key_grad_own[:keep_rows], key_grad_own + returned[0]], axis=0)
    value_grad_own = jnp.concatenate(
        [value_grad_own[:keep_rows], value_grad_own + returned[1]], axis=0
    )

    def query_shape(raw_proj):
        return norm_rope(raw_proj, query_gain, cosines, sines)

    def key_shape(raw_proj):
        return norm_rope(raw_proj, key_gain, cosines, sines)

    query_back = jax.vjp(query_shape, query_raw)[1](query_grad.reshape(row_count, -1, head_size))[
        0
    ].astype(jnp.bfloat16)
    key_back = jax.vjp(key_shape, key_raw)[1](key_grad_own)[0].astype(jnp.bfloat16)
    value_back = value_grad_own.reshape(row_count, kv_cols).astype(jnp.bfloat16)
    out_part = jnp.dot(attended_flat, output_weight, preferred_element_type=jnp.float32)
    query_rows = query_back
    key_rows = key_back
    value_rows = value_back
    summed = jnp.einsum("nh,dh->nd", query_rows, query_weight, preferred_element_type=jnp.float32)
    summed = summed + jnp.einsum(
        "nh,dh->nd", key_rows, key_weight, preferred_element_type=jnp.float32
    )
    summed = summed + jnp.einsum(
        "nh,dh->nd", value_rows, value_weight, preferred_element_type=jnp.float32
    )
    out_sum, grad_sum = (
        lax.psum_scatter(
            out_part.astype(jnp.bfloat16), "tp", scatter_dimension=0, tiled=True
        ).astype(jnp.float32),
        lax.psum_scatter(summed.astype(jnp.bfloat16), "tp", scatter_dimension=0, tiled=True).astype(
            jnp.float32
        ),
    )
    layer_output = (tokens.astype(jnp.float32) + out_sum).astype(jnp.bfloat16)
    tokens_grad = (result_grad.astype(jnp.float32) + grad_sum).astype(jnp.bfloat16)
    return (layer_output, tokens_grad)


def solution(mesh):
    in_specs = (
        P(("ctx", "tp"), None),
        P(("ctx", "tp"), None),
        P(None, "tp"),
        P(None, "tp"),
        P(None, "tp"),
        P("tp", None),
        P(),
        P(),
    )
    out_specs = (P(("ctx", "tp"), None), P(("ctx", "tp"), None))
    return jax.shard_map(
        on_device, mesh=mesh, in_specs=in_specs, out_specs=out_specs, check_vma=False
    )
```

profile of v0, /device:TPU:13, one launch (start us, length us, event | category | flops | bytes accessed | tf_op | source)
XLA Modules:
  0.0 91.3 jit_solution(1839996132509159438)
XLA Ops:
  7.2 2.7 %pad_maximum_fusion = bf16[2,128,2688]{2,1,0:T(8,128)(2,1)} fusion(bf16[1,128,2688]{2,1,0:T(8,128)(2,1)} %bitcast.158, bf16[1,128,2688]{2,1,0:T(8,128)(2,1)} %bitcast.157), kind=kLoop, calls=%fused_computation.20 | loop fusion | flops 688128 | bytes 2752512 | tf_op jit(solution)/shard_map/stack | solution.py:90
  10.0 1.3 %copy-done.1 = bf16[2688,256]{1,0:T(8,128)(2,1)S(1)} copy-done((bf16[2688,256]{1,0:T(8,128)(2,1)S(1)}, bf16[2688,256]{1,0:T(8,128)(2,1)}, u32[]{:S(2)}) %copy-start.1) | copy-done | bytes 1376280
  11.2 1.7 %copy.30 = bf16[256,2688]{1,0:T(8,128)(2,1)} copy(bf16[256,2688]{0,1:T(8,128)(2,1)S(1)} %bitcast.156) | data formatting | bytes 2752512 | tf_op jit(solution)/shard_map/dot_general | solution.py:94
  13.3 1.6 %fusion.20 = pred[256,1280]{0,1:T(8,128)(4,1)} fusion(s32[1280]{0:T(1024)S(1)} %iota_add_fusion, s32[256]{0:T(256)S(1)} %iota_add_fusion.1, pred[1280]{0:T(1024)(128)(4,1)S(1)} %broadcast_compare_fusion), kind=kLoop, calls=%fused_computation.34 | loop fusion | flops 1638400 | bytes 335104 | tf_op jit(solution)/shard_map/and | solution.py:55
  14.9 8.6 %all-gather.2.cloned.1.call-done = bf16[2,256,2688]{2,1,0:T(8,128)(2,1)} async-done(((bf16[2,128,2688]{2,1,0:T(8,128)(2,1)}), bf16[2,256,2688]{2,1,0:T(8,128)(2,1)}) %all-gather.2.cloned.1.call-update) | async-done | bytes 2752528 | tf_op jit(solution)/shard_map/all_gather | solution.py:91
  23.4 2.3 %multiply_reduce_fusion.2 = (f32[256]{0:T(256)S(1)}, f32[256,128]{0,1:T(8,128)S(1)}) fusion(bf16[2688,128]{1,0:T(8,128)(2,1)} %param.11, bf16[2,256,2688]{2,1,0:T(8,128)(2,1)} %all-gather.2.cloned.1.call-done), kind=kOutput, calls=%fused_computation.77 | convolution fusion | flops 176226048 | bytes 2196480 | tf_op jit(solution)/shard_map/dot_general | solution.py:95
  26.2 2.0 %fusion.28 = bf16[256,128]{0,1:T(8,128)(2,1)S(1)} fusion(bf16[2688,128]{1,0:T(8,128)(2,1)S(1)} %copy-done.8, bf16[2,256,2688]{2,1,0:T(8,128)(2,1)} %all-gather.2.cloned.1.call-done), kind=kOutput, calls=%fused_computation.39 | convolution fusion | flops 176193536 | bytes 2129920 | tf_op jit(solution)/shard_map/dot_general | solution.py:96
  28.2 3.1 %collective-permute-start.3 = (bf16[2,256,1,128]{1,3,2,0:T(8,128)(2,1)S(1)}, bf16[2,256,1,128]{1,3,2,0:T(8,128)(2,1)S(1)}, u32[]{:S(2)}, u32[]{:S(2)}) collective-permute-start(bf16[2,256,1,128]{1,3,2,0:T(8,128)(2,1)S(1)} %pad_maximum_fusion.1), channel_id=1, source_target_pairs={{0,2},{2,4},{4,6},{6,8},{8,10},{10,12},{12,14},{14,16},{16,18},{18... | collective-permute-start | bytes 393224 | tf_op jit(solution)/shard_map/ppermute | solution.py:17
  31.4 3.1 %collective-permute-start.2 = (bf16[2,256,1,128]{1,3,2,0:T(8,128)(2,1)S(1)}, bf16[2,256,1,128]{1,3,2,0:T(8,128)(2,1)S(1)}, u32[]{:S(2)}, u32[]{:S(2)}) collective-permute-start(bf16[2,256,1,128]{1,3,2,0:T(8,128)(2,1)S(1)} %pad_maximum_fusion.1), channel_id=1, source_target_pairs={{0,4},{2,6},{4,8},{6,10},{8,12},{10,14},{12,16},{14,18},{16,20},{1... | collective-permute-start | bytes 393224 | tf_op jit(solution)/shard_map/ppermute | solution.py:17
  34.5 4.0 %collective-permute-start.1 = (bf16[2,256,1,128]{1,3,2,0:T(8,128)(2,1)S(1)}, bf16[2,256,1,128]{1,3,2,0:T(8,128)(2,1)S(1)}, u32[]{:S(2)}, u32[]{:S(2)}) collective-permute-start(bf16[2,256,1,128]{1,3,2,0:T(8,128)(2,1)S(1)} %pad_maximum_fusion.1), channel_id=1, source_target_pairs={{0,6},{2,8},{4,10},{6,12},{8,14},{10,16},{12,18},{14,20},{16,22},{... | collective-permute-start | bytes 393224 | tf_op jit(solution)/shard_map/ppermute | solution.py:17
  38.5 1.9 %collective-permute-start = (bf16[2,256,1,128]{1,3,2,0:T(8,128)(2,1)S(1)}, bf16[2,256,1,128]{1,3,2,0:T(8,128)(2,1)S(1)}, u32[]{:S(2)}, u32[]{:S(2)}) collective-permute-start(bf16[2,256,1,128]{1,3,2,0:T(8,128)(2,1)S(1)} %pad_maximum_fusion.1), channel_id=1, source_target_pairs={{0,8},{2,10},{4,12},{6,14},{8,16},{10,18},{12,20},{14,22},{16,24},... | collective-permute-start | bytes 393224 | tf_op jit(solution)/shard_map/ppermute | solution.py:17
  40.5 0.6 multiply_reduce_fusion.1
  41.8 2.4 %collective-permute-done = bf16[2,256,1,128]{1,3,2,0:T(8,128)(2,1)S(1)} collective-permute-done((bf16[2,256,1,128]{1,3,2,0:T(8,128)(2,1)S(1)}, bf16[2,256,1,128]{1,3,2,0:T(8,128)(2,1)S(1)}, u32[]{:S(2)}, u32[]{:S(2)}) %collective-permute-start) | collective-permute-done | bytes 131104 | tf_op jit(solution)/shard_map/ppermute | solution.py:17
  44.3 0.8 fusion.73
  48.0 0.8 fusion.72
  48.9 1.7 %convolution_convert_fusion = bf16[256,2688]{1,0:T(8,128)(2,1)} fusion(bf16[256,256]{0,1:T(8,128)(2,1)S(1)} %bitcast.160, bf16[256,2688]{1,0:T(8,128)(2,1)S(1)} %copy-done), kind=kOutput, calls=%fused_computation.3 | convolution fusion | flops 353009664 | bytes 2883584 | tf_op jit(solution)/shard_map/dot_general | solution.py:165
  50.6 2.5 %collective-permute-start.4 = (bf16[2,256,1,128]{1,3,2,0:T(8,128)(2,1)}, bf16[2,256,1,128]{1,3,2,0:T(8,128)(2,1)S(1)}, u32[]{:S(2)}, u32[]{:S(2)}) collective-permute-start(bf16[2,256,1,128]{1,3,2,0:T(8,128)(2,1)} %get-tuple-element.2), channel_id=1, source_target_pairs={{2,0},{4,2},{6,4},{8,6},{10,8},{12,10},{14,12},{16,14},{18,16},{20... | collective-permute-start | bytes 393224 | tf_op jit(solution)/shard_map/ppermute | solution.py:17
  53.1 1.9 %collective-permute-start.7 = (bf16[2,256,1,128]{1,3,2,0:T(8,128)(2,1)}, bf16[2,256,1,128]{1,3,2,0:T(8,128)(2,1)S(1)}, u32[]{:S(2)}, u32[]{:S(2)}) collective-permute-start(bf16[2,256,1,128]{1,3,2,0:T(8,128)(2,1)} %get-tuple-element.3), channel_id=1, source_target_pairs={{8,0},{10,2},{12,4},{14,6},{16,8},{18,10},{20,12},{22,14},{24,16},... | collective-permute-start | bytes 393224 | tf_op jit(solution)/shard_map/ppermute | solution.py:17
  55.1 1.9 %collective-permute-start.6 = (bf16[2,256,1,128]{1,3,2,0:T(8,128)(2,1)}, bf16[2,256,1,128]{1,3,2,0:T(8,128)(2,1)S(1)}, u32[]{:S(2)}, u32[]{:S(2)}) collective-permute-start(bf16[2,256,1,128]{1,3,2,0:T(8,128)(2,1)} %get-tuple-element.4), channel_id=1, source_target_pairs={{6,0},{8,2},{10,4},{12,6},{14,8},{16,10},{18,12},{20,14},{22,16},{... | collective-permute-start | bytes 393224 | tf_op jit(solution)/shard_map/ppermute | solution.py:17
  57.0 2.4 %collective-permute-start.5 = (bf16[2,256,1,128]{1,3,2,0:T(8,128)(2,1)}, bf16[2,256,1,128]{1,3,2,0:T(8,128)(2,1)S(1)}, u32[]{:S(2)}, u32[]{:S(2)}) collective-permute-start(bf16[2,256,1,128]{1,3,2,0:T(8,128)(2,1)} %get-tuple-element.5), channel_id=1, source_target_pairs={{4,0},{6,2},{8,4},{10,6},{12,8},{14,10},{16,12},{18,14},{20,16},{2... | collective-permute-start | bytes 393224 | tf_op jit(solution)/shard_map/ppermute | solution.py:17
  59.4 0.8 multiply_reduce_fusion
  60.1 0.8 fusion.35
  60.9 0.6 fusion.74
  61.6 2.5 %collective-permute-done.6 = bf16[2,256,1,128]{1,3,2,0:T(8,128)(2,1)S(1)} collective-permute-done((bf16[2,256,1,128]{1,3,2,0:T(8,128)(2,1)}, bf16[2,256,1,128]{1,3,2,0:T(8,128)(2,1)S(1)}, u32[]{:S(2)}, u32[]{:S(2)}) %collective-permute-start.6) | collective-permute-done | bytes 131104 | tf_op jit(solution)/shard_map/ppermute | solution.py:17
  64.1 2.0 %collective-permute-done.5 = bf16[2,256,1,128]{1,3,2,0:T(8,128)(2,1)S(1)} collective-permute-done((bf16[2,256,1,128]{1,3,2,0:T(8,128)(2,1)}, bf16[2,256,1,128]{1,3,2,0:T(8,128)(2,1)S(1)}, u32[]{:S(2)}, u32[]{:S(2)}) %collective-permute-start.5) | collective-permute-done | bytes 131104 | tf_op jit(solution)/shard_map/ppermute | solution.py:17
  66.1 0.9 %fusion.40 = f32[256,1,128]{0,2,1:T(8,128)S(1)} fusion(f32[2,256,1,128]{1,3,2,0:T(8,128)S(1)} %convert_add_fusion, f32[1280,1,128]{0,2,1:T(8,128)} %copy-done.5), kind=kLoop, calls=%fused_computation.66 | loop fusion | flops 32768 | bytes 393216 | tf_op jit(solution)/shard_map/add | solution.py:149
  67.6 0.6 convolution_add_fusion.1
  68.7 2.5 %fusion = bf16[256,2688]{1,0:T(8,128)(2,1)} fusion(f32[256,2688]{1,0:T(8,128)S(1)} %convolution_add_fusion.1, bf16[2688,128]{1,0:T(8,128)(2,1)S(1)} %copy-done.9, f32[2,256,1,128]{1,3,2,0:T(8,128)S(1)} %convert_add_fusion, f32[1280,1,128]{0,2,1:T(8,128)} %copy-done.4), kind=kOutput, calls=%fused_computation.2 | convolution fusion | flops 177602560 | bytes 5079040 | tf_op jit(solution)/shard_map/nh,dh->nd/dot_general | solution.py:173
  71.3 1.0 %copy-done.2 = bf16[128,2688]{1,0:T(8,128)(2,1)S(1)} copy-done((bf16[128,2688]{1,0:T(8,128)(2,1)S(1)}, bf16[128,2688]{1,0:T(8,128)(2,1)}, u32[]{:S(2)}) %copy-start.2) | copy-done | bytes 688152
  72.3 2.1 %add_convert_fusion.1 = bf16[128,2688]{1,0:T(8,128)(2,1)} fusion(bf16[128,2688]{1,0:T(8,128)(2,1)} %reduce-scatter.3.cloned.1.call-done, bf16[128,2688]{1,0:T(8,128)(2,1)S(1)} %copy-done.2), kind=kLoop, calls=%fused_computation.28 | loop fusion | flops 1376256 | bytes 2064384 | tf_op jit(solution)/shard_map/convert_element_type | solution.py:184
  74.4 8.3 %reduce-scatter.5.cloned.1.call-done = bf16[128,2688]{1,0:T(8,128)(2,1)} async-done(((bf16[256,2688]{1,0:T(8,128)(2,1)}), bf16[128,2688]{1,0:T(8,128)(2,1)}) %reduce-scatter.5.cloned.1.call-update) | async-done | bytes 688144 | tf_op jit(solution)/shard_map/reduce_scatter | solution.py:180
  82.7 2.1 %add_convert_fusion = bf16[128,2688]{1,0:T(8,128)(2,1)} fusion(bf16[128,2688]{1,0:T(8,128)(2,1)} %reduce-scatter.5.cloned.1.call-done, bf16[128,2688]{1,0:T(8,128)(2,1)S(1)} %copy-done.3), kind=kLoop, calls=%fused_computation.27 | loop fusion | flops 1376256 | bytes 2064384 | tf_op jit(solution)/shard_map/convert_element_type | solution.py:185
  (82 shorter events, 5.7 us)
Async XLA Ops:
  7.2 34.0 %copy-start = (bf16[256,2688]{1,0:T(8,128)(2,1)S(1)}, bf16[256,2688]{1,0:T(8,128)(2,1)}, u32[]{:S(2)}) copy-start(bf16[256,2688]{1,0:T(8,128)(2,1)} %param.13) | copy-start | bytes 4128772
  7.2 16.3 %all-gather.2.cloned.1.call-start = ((), (), s32[]{:S(2)}) async-start(), calls=%async_computation.2 | async-start | bytes 4128768 | tf_op jit(solution)/shard_map/all_gather | solution.py:91
  9.9 1.3 %copy-start.1 = (bf16[2688,256]{1,0:T(8,128)(2,1)S(1)}, bf16[2688,256]{1,0:T(8,128)(2,1)}, u32[]{:S(2)}) copy-start(bf16[2688,256]{1,0:T(8,128)(2,1)} %param.10) | copy-start | bytes 4128772
  9.9 61.4 %reduce-scatter.3.cloned.1.call-start = ((), (), s32[]{:S(2)}) async-start(), calls=%async_computation.3 | async-start | bytes 2064384 | tf_op jit(solution)/shard_map/reduce_scatter | solution.py:177
  12.9 13.0 %copy-start.13 = (f32[64]{0:T(128)}, f32[64]{0:T(128)S(1)}, u32[]{:S(2)}) copy-start(f32[64]{0:T(128)S(1)} %negate_power_fusion) | copy-start | bytes 772
  12.9 12.8 %copy-start.11 = (f32[128]{0:T(128)S(1)}, f32[128]{0:T(128)}, u32[]{:S(2)}) copy-start(f32[128]{0:T(128)} %param.15) | copy-start | bytes 1540
  23.4 2.8 %copy-start.8 = (bf16[2688,128]{1,0:T(8,128)(2,1)S(1)}, bf16[2688,128]{1,0:T(8,128)(2,1)}, u32[]{:S(2)}) copy-start(bf16[2688,128]{1,0:T(8,128)(2,1)} %param.12) | copy-start | bytes 2064388
  23.4 17.0 %copy-start.18 = (bf16[2,256,2688]{2,1,0:T(8,128)(2,1)S(1)}, bf16[2,256,2688]{2,1,0:T(8,128)(2,1)}, u32[]{:S(2)}) copy-start(bf16[2,256,2688]{2,1,0:T(8,128)(2,1)} %all-gather.2.cloned.1.call-done) | copy-start | bytes 8257540
  25.7 2.5 %copy-start.16 = (f32[256]{0:T(256)}, f32[256]{0:T(256)S(1)}, u32[]{:S(2)}) copy-start(f32[256]{0:T(256)S(1)} %get-tuple-element.18) | copy-start | bytes 3076
  25.9 14.6 %copy-start.6 = (bf16[256,2688]{1,0:T(8,128)(2,1)S(1)}, bf16[256,2688]{1,0:T(8,128)(2,1)}, u32[]{:S(2)}) copy-start(bf16[256,2688]{1,0:T(8,128)(2,1)} %copy.30) | copy-start | bytes 4128772
  28.2 16.0 %collective-permute-start.3 = (bf16[2,256,1,128]{1,3,2,0:T(8,128)(2,1)S(1)}, bf16[2,256,1,128]{1,3,2,0:T(8,128)(2,1)S(1)}, u32[]{:S(2)}, u32[]{:S(2)}) collective-permute-start(bf16[2,256,1,128]{1,3,2,0:T(8,128)(2,1)S(1)} %pad_maximum_fusion.1), channel_id=1, source_target_pairs={{0,2},{2,4},{4,6},{6,8},{8,10},{10,12},{12,14},{14,16},{16,18},{18... | collective-permute-start | bytes 393224 | tf_op jit(solution)/shard_map/ppermute | solution.py:17
  31.4 12.9 %collective-permute-start.2 = (bf16[2,256,1,128]{1,3,2,0:T(8,128)(2,1)S(1)}, bf16[2,256,1,128]{1,3,2,0:T(8,128)(2,1)S(1)}, u32[]{:S(2)}, u32[]{:S(2)}) collective-permute-start(bf16[2,256,1,128]{1,3,2,0:T(8,128)(2,1)S(1)} %pad_maximum_fusion.1), channel_id=1, source_target_pairs={{0,4},{2,6},{4,8},{6,10},{8,12},{10,14},{12,16},{14,18},{16,20},{1... | collective-permute-start | bytes 393224 | tf_op jit(solution)/shard_map/ppermute | solution.py:17
  34.5 9.7 %collective-permute-start.1 = (bf16[2,256,1,128]{1,3,2,0:T(8,128)(2,1)S(1)}, bf16[2,256,1,128]{1,3,2,0:T(8,128)(2,1)S(1)}, u32[]{:S(2)}, u32[]{:S(2)}) collective-permute-start(bf16[2,256,1,128]{1,3,2,0:T(8,128)(2,1)S(1)} %pad_maximum_fusion.1), channel_id=1, source_target_pairs={{0,6},{2,8},{4,10},{6,12},{8,14},{10,16},{12,18},{14,20},{16,22},{... | collective-permute-start | bytes 393224 | tf_op jit(solution)/shard_map/ppermute | solution.py:17
  38.5 5.7 %collective-permute-start = (bf16[2,256,1,128]{1,3,2,0:T(8,128)(2,1)S(1)}, bf16[2,256,1,128]{1,3,2,0:T(8,128)(2,1)S(1)}, u32[]{:S(2)}, u32[]{:S(2)}) collective-permute-start(bf16[2,256,1,128]{1,3,2,0:T(8,128)(2,1)S(1)} %pad_maximum_fusion.1), channel_id=1, source_target_pairs={{0,8},{2,10},{4,12},{6,14},{8,16},{10,18},{12,20},{14,22},{16,24},... | collective-permute-start | bytes 393224 | tf_op jit(solution)/shard_map/ppermute | solution.py:17
  40.4 0.7 copy-start.15
  41.8 2.6 %copy-start.10 = (pred[256,1280]{0,1:T(8,128)(4,1)S(1)}, pred[256,1280]{0,1:T(8,128)(4,1)}, u32[]{:S(2)}) copy-start(pred[256,1280]{0,1:T(8,128)(4,1)} %fusion.20) | copy-start | bytes 983044
  45.9 1.9 %copy-start.4 = (f32[1280,1,128]{0,2,1:T(8,128)}, f32[1280,1,128]{0,2,1:T(8,128)S(1)}, u32[]{:S(2)}) copy-start(f32[1280,1,128]{0,2,1:T(8,128)S(1)} %convolution_bitcast_fusion.1) | copy-start | bytes 1966084
  47.9 1.0 %copy-start.5 = (f32[1280,1,128]{0,2,1:T(8,128)}, f32[1280,1,128]{0,2,1:T(8,128)S(1)}, u32[]{:S(2)}) copy-start(f32[1280,1,128]{0,2,1:T(8,128)S(1)} %convolution_bitcast_fusion.2) | copy-start | bytes 1966084
  50.5 32.1 %reduce-scatter.5.cloned.1.call-start = ((), (), s32[]{:S(2)}) async-start(), calls=%async_computation.4 | async-start | bytes 2064384 | tf_op jit(solution)/shard_map/reduce_scatter | solution.py:180
  50.6 10.9 %collective-permute-start.4 = (bf16[2,256,1,128]{1,3,2,0:T(8,128)(2,1)}, bf16[2,256,1,128]{1,3,2,0:T(8,128)(2,1)S(1)}, u32[]{:S(2)}, u32[]{:S(2)}) collective-permute-start(bf16[2,256,1,128]{1,3,2,0:T(8,128)(2,1)} %get-tuple-element.2), channel_id=1, source_target_pairs={{2,0},{4,2},{6,4},{8,6},{10,8},{12,10},{14,12},{16,14},{18,16},{20... | collective-permute-start | bytes 393224 | tf_op jit(solution)/shard_map/ppermute | solution.py:17
  53.1 8.5 %collective-permute-start.7 = (bf16[2,256,1,128]{1,3,2,0:T(8,128)(2,1)}, bf16[2,256,1,128]{1,3,2,0:T(8,128)(2,1)S(1)}, u32[]{:S(2)}, u32[]{:S(2)}) collective-permute-start(bf16[2,256,1,128]{1,3,2,0:T(8,128)(2,1)} %get-tuple-element.3), channel_id=1, source_target_pairs={{8,0},{10,2},{12,4},{14,6},{16,8},{18,10},{20,12},{22,14},{24,16},... | collective-permute-start | bytes 393224 | tf_op jit(solution)/shard_map/ppermute | solution.py:17
  55.1 9.0 %collective-permute-start.6 = (bf16[2,256,1,128]{1,3,2,0:T(8,128)(2,1)}, bf16[2,256,1,128]{1,3,2,0:T(8,128)(2,1)S(1)}, u32[]{:S(2)}, u32[]{:S(2)}) collective-permute-start(bf16[2,256,1,128]{1,3,2,0:T(8,128)(2,1)} %get-tuple-element.4), channel_id=1, source_target_pairs={{6,0},{8,2},{10,4},{12,6},{14,8},{16,10},{18,12},{20,14},{22,16},{... | collective-permute-start | bytes 393224 | tf_op jit(solution)/shard_map/ppermute | solution.py:17
  57.0 9.1 %collective-permute-start.5 = (bf16[2,256,1,128]{1,3,2,0:T(8,128)(2,1)}, bf16[2,256,1,128]{1,3,2,0:T(8,128)(2,1)S(1)}, u32[]{:S(2)}, u32[]{:S(2)}) collective-permute-start(bf16[2,256,1,128]{1,3,2,0:T(8,128)(2,1)} %get-tuple-element.5), channel_id=1, source_target_pairs={{4,0},{6,2},{8,4},{10,6},{12,8},{14,10},{16,12},{18,14},{20,16},{2... | collective-permute-start | bytes 393224 | tf_op jit(solution)/shard_map/ppermute | solution.py:17
  60.9 6.2 %copy-start.14 = (f32[64]{0:T(128)S(1)}, f32[64]{0:T(128)}, u32[]{:S(2)}) copy-start(f32[64]{0:T(128)} %copy-done.13) | copy-start | bytes 772
  61.5 5.9 %copy-start.12 = (f32[128]{0:T(128)S(1)}, f32[128]{0:T(128)}, u32[]{:S(2)}) copy-start(f32[128]{0:T(128)} %param.15) | copy-start | bytes 1540
  61.6 6.0 %copy-start.17 = (f32[256]{0:T(256)S(1)}, f32[256]{0:T(256)}, u32[]{:S(2)}) copy-start(f32[256]{0:T(256)} %copy-done.16) | copy-start | bytes 3076
  61.6 6.0 %copy-start.7 = (bf16[2688,128]{1,0:T(8,128)(2,1)S(1)}, bf16[2688,128]{1,0:T(8,128)(2,1)}, u32[]{:S(2)}) copy-start(bf16[2688,128]{1,0:T(8,128)(2,1)} %param.11) | copy-start | bytes 2064388
  67.6 1.1 %copy-start.9 = (bf16[2688,128]{1,0:T(8,128)(2,1)S(1)}, bf16[2688,128]{1,0:T(8,128)(2,1)}, u32[]{:S(2)}) copy-start(bf16[2688,128]{1,0:T(8,128)(2,1)} %param.12) | copy-start | bytes 2064388
  71.2 1.1 %copy-start.2 = (bf16[128,2688]{1,0:T(8,128)(2,1)S(1)}, bf16[128,2688]{1,0:T(8,128)(2,1)}, u32[]{:S(2)}) copy-start(bf16[128,2688]{1,0:T(8,128)(2,1)} %param.8) | copy-start | bytes 2064388
  71.2 11.5 %copy-start.3 = (bf16[128,2688]{1,0:T(8,128)(2,1)S(1)}, bf16[128,2688]{1,0:T(8,128)(2,1)}, u32[]{:S(2)}) copy-start(bf16[128,2688]{1,0:T(8,128)(2,1)} %param.9) | copy-start | bytes 2064388
Sparse Core Ops, SparseCore 0:
  10.0 13.3 all-gather.1
  50.7 10.2 reduce-scatter.2
  71.4 11.2 reduce-scatter.4
where the time goes:
time: 92.8 us; the launch traced here: 91.3 us
  waiting for transfers between devices  23.8 us (26%)
  starting transfers between devices  21 us (23%)
  between operations  14.3 us (15%)
  matrix products  14 us (15%)
  other arithmetic  12.8 us (14%)
  local copies, waits for them, and re-layouts  5.53 us (6%)
    ppermute x8, starting transfers between devices, from_behind(): return lax.ppermute(block, axis, route)  20.8 us
    all_gather x1, waiting for transfers between devices, on_device(): portion = lax.all_gather(stacked, 'tp', axis=1, tiled=True)  8.57 us
    reduce_scatter x1, waiting for transfers between devices, on_device(): lax.psum_scatter(summed.astype(jnp.bfloat16), 'tp', scatter_dimension=0,...  8.28 us
    ppermute x8, waiting for transfers between devices, from_behind(): return lax.ppermute(block, axis, route)  6.84 us
    unnamed x41, local copies, waits for them, and re-layouts  2.91 us
    another operation x1, other arithmetic, on_device(): stacked = jnp.stack([tokens, result_grad])  2.66 us
    dot_general x1, matrix products, on_device(): jnp.einsum('nh,dh->nd', value_rows, value_weight, preferred_element_type=...  2.54 us
    dot_general x1, matrix products, on_device(): jnp.dot(inputs_part, key_weight, preferred_element_type=jnp.float32)  2.27 us
  transfers between devices with their start and end apart: 11, of which 5 were waited for; matrix products, arithmetic and copies ran while one was open for 15% of the time, Pallas kernels for 0%

commit v1 on v0

v1 whole, which is shorter than its diff:
```python
import functools

import jax
import jax.numpy as jnp
from jax import lax
from jax.experimental import pallas as pl
from jax.experimental.pallas import tpu as pltpu
from jax.sharding import PartitionSpec as P

WINDOW = 1024
norm_epsilon = 1e-06
score_scale = 168.0 ** (-0.5)
rope_theta = 10000.0
MESH = pl.DeviceIdType.MESH
f32 = jnp.float32
bf16 = jnp.bfloat16


def dot(a, b, ca, cb):
    return lax.dot_general(a, b, (((ca,), (cb,)), ((), ())), preferred_element_type=f32)


def rope(n, cosines, sines, half):
    return n * cosines + pltpu.roll(n, half, 1) * sines


def rope_back(g, cosines, sines, half):
    return g * cosines + pltpu.roll(g * sines, half, 1)


def inverse_rms(u):
    return lax.rsqrt(jnp.mean(u * u, axis=-1, keepdims=True) + norm_epsilon)


def norm_rope_back(g, u, gain, cosines, sines, half):
    r = inverse_rms(u)
    w = rope_back(g, cosines, sines, half) * gain
    return r * (w - u * (r * r * jnp.mean(w * u, axis=-1, keepdims=True)))


def kernel(
    n_ctx, n_tp, reach, per_kv, kv_count, head, tile,
    tokens, rgrad, qw, kw, vw, ow, qgain, kgain, freq,
    out_ref, gout_ref,
    wqkv, wo, xg, gg, raw, cos_t, sin_t, q_s, do_s, dot_s, kv_own, halo, e_s, dp_s,
    l_s, ot_s, dqt_s, att, dkv, sum4, own_grad, gin, rin, zbuf, back, part, rs_in, stage,
    local_sem, ag_send, ag_recv, f_send, f_relay, f_recv, b_send, g_recv, r_recv,
    rs_send, rs_recv, out_sem,
):
    c = lax.axis_index("ctx")
    t = lax.axis_index("tp")
    s = lax.rem(c, reach)
    z = lax.div(c, reach)
    nz = n_ctx // reach
    local, width = xg.shape[1], xg.shape[2]
    rows = local * n_tp
    half = head // 2
    qc = kv_count * per_kv * head
    kc = kv_count * head
    qn = per_kv * rows

    def local_copy(i, src, dst):
        return pltpu.make_async_copy(src, dst, local_sem.at[i])

    loads = [
        local_copy(0, tokens, xg.at[t]),
        local_copy(1, kw, wqkv.at[:, qc : qc + kc]),
        local_copy(2, vw, wqkv.at[:, qc + kc : qc + 2 * kc]),
        local_copy(3, qw, wqkv.at[:, :qc]),
        local_copy(4, rgrad, gg.at[t]),
        local_copy(5, ow, wo),
    ]
    for load in loads:
        load.start()

    def to_ctx(src, dst, send, recv, target):
        return pltpu.make_async_remote_copy(
            src_ref=src, dst_ref=dst, send_sem=send, recv_sem=recv,
            device_id={"ctx": target}, device_id_type=MESH,
        )

    def to_tp(src, dst, send, recv, target):
        return pltpu.make_async_remote_copy(
            src_ref=src, dst_ref=dst, send_sem=send, recv_sem=recv,
            device_id={"tp": target}, device_id_type=MESH,
        )

    barrier = pltpu.get_barrier_semaphore()
    for j in range(1, n_tp):
        pl.semaphore_signal(
            barrier, inc=1, device_id={"tp": lax.rem(t + j, n_tp)}, device_id_type=MESH
        )
    for j in range(1, reach):
        mate = z * reach + lax.rem(s + j, reach)
        pl.semaphore_signal(barrier, inc=1, device_id={"ctx": mate}, device_id_type=MESH)

    @pl.when(z + 1 < nz)
    def _():
        pl.semaphore_signal(barrier, inc=1, device_id={"ctx": c + reach}, device_id_type=MESH)

    @pl.when(z > 0)
    def _():
        pl.semaphore_signal(barrier, inc=1, device_id={"ctx": c - reach}, device_id_type=MESH)

    greeted = (
        n_tp - 1 + reach - 1
        + jnp.where(z > 0, jnp.int32(1), jnp.int32(0))
        + jnp.where(z + 1 < nz, jnp.int32(1), jnp.int32(0))
    )
    pl.semaphore_wait(barrier, greeted)

    gathers = []
    for w, (src, dst) in enumerate(((tokens, xg), (rgrad, gg))):
        for j in range(1, n_tp):
            copy = to_tp(src, dst.at[t], ag_send.at[w, j - 1], ag_recv.at[w, j - 1],
                         lax.rem(t + j, n_tp))
            copy.start()
            gathers.append((w, copy))

    position = (c * rows + lax.broadcasted_iota(jnp.int32, (rows, head), 0)).astype(f32)
    angles = position * freq[...]
    lane = lax.broadcasted_iota(jnp.int32, (rows, head), 1)
    cos_t[...] = jnp.cos(angles)
    sines = jnp.sin(angles)
    sin_t[...] = jnp.where(lane < half, -sines, sines)

    for i in (0, 1, 2):
        loads[i].wait()
    for w, copy in gathers:
        if w == 0:
            copy.wait_recv()
    x_all = xg[...].reshape(rows, width)
    raw[:, qc : qc + 2 * kc] = dot(x_all, wqkv[:, qc : qc + 2 * kc], 1, 0)
    for m in range(kv_count):
        u = raw[:, qc + m * head : qc + (m + 1) * head]
        n = u * inverse_rms(u) * kgain[...]
        kv_own[0, m] = rope(n, cos_t[...], sin_t[...], half).astype(bf16)
        v0 = qc + kc + m * head
        kv_own[1, m] = raw[:, v0 : v0 + head].astype(bf16)

    def ahead():
        return to_ctx(kv_own, halo.at[reach - 1], f_send.at[reach - 1], f_recv.at[reach - 1],
                      c + reach)

    def own_to(k):
        return to_ctx(kv_own, halo.at[k - 1], f_send.at[k - 1], f_recv.at[k - 1], c + k)

    def relay_to(k):
        return to_ctx(halo.at[reach - 1], halo.at[reach - k - 1], f_relay.at[k - 1],
                      f_recv.at[reach - k - 1], c - k)

    def halo_wait(d):
        to_ctx(kv_own, halo.at[d - 1], f_send.at[d - 1], f_recv.at[d - 1], c).wait_recv()

    @pl.when(z + 1 < nz)
    def _():
        ahead().start()

    for k in range(1, reach):
        @pl.when(s + k < reach)
        def _(k=k):
            own_to(k).start()

    loads[3].wait()
    raw[:, :qc] = dot(xg[...].reshape(rows, width), wqkv[:, :qc], 1, 0)
    for h in range(kv_count * per_kv):
        m, g = h // per_kv, h % per_kv
        u = raw[:, h * head : (h + 1) * head]
        n = u * inverse_rms(u) * qgain[...]
        q_s[m, g * rows : (g + 1) * rows] = rope(n, cos_t[...], sin_t[...], half).astype(bf16)
    loads[4].wait()
    loads[5].wait()
    for w, copy in gathers:
        if w == 1:
            copy.wait_recv()
    d_out = dot(gg[...].reshape(rows, width), wo[...], 1, 1).astype(bf16)
    for h in range(kv_count * per_kv):
        m, g = h // per_kv, h % per_kv
        piece = d_out[:, h * head : (h + 1) * head]
        do_s[m, g * rows : (g + 1) * rows] = piece
        dot_s[m, :, g * rows : (g + 1) * rows] = piece.astype(f32).T

    def kv(d, w, m):
        return kv_own[w, m] if d == 0 else halo[d - 1, w, m]

    def first_pass(d):
        for m in range(kv_count):
            key, value = kv(d, 0, m), kv(d, 1, m)
            e = jnp.exp(dot(key, q_s[m], 1, 1) * score_scale)
            if d == 0 or d == reach:
                key_row = lax.broadcasted_iota(jnp.int32, (rows, qn), 0)
                query_row = lax.broadcasted_iota(jnp.int32, (rows, qn), 1) % rows
                keep = query_row >= key_row if d == 0 else query_row < key_row
                e = jnp.where(keep, e, f32(0.0))
            total = jnp.sum(e, axis=0, keepdims=True)
            low = e.astype(bf16)
            e_s[d, m] = low
            mixed = dot(value, low, 0, 0)
            dp_s[d, m] = dot(value, do_s[m], 1, 1) * score_scale
            if d == 0:
                l_s[m] = total
                ot_s[m] = mixed
            else:
                l_s[m] += total
                ot_s[m] += mixed

    first_pass(0)

    @pl.when(z > 0)
    def _():
        halo_wait(reach)
        for k in range(1, reach):
            @pl.when(k <= s)
            def _(k=k):
                relay_to(k).start()
        first_pass(reach)

    for d in range(1, reach):
        @pl.when(c >= d)
        def _(d=d):
            halo_wait(d)
            first_pass(d)

    inv, delta = [], []
    for m in range(kv_count):
        inv.append(1.0 / l_s[m])
        o_t = (ot_s[m] * inv[m]).astype(bf16).astype(f32)
        delta.append(jnp.sum(o_t * dot_s[m], axis=0, keepdims=True) * score_scale)
        for g in range(per_kv):
            h = m * per_kv + g
            att[:, h * head : (h + 1) * head] = o_t[:, g * rows : (g + 1) * rows].T.astype(bf16)
        l_s[m] = inv[m]
        dqt_s[m] = jnp.zeros_like(dqt_s[m])

    def second_pass(d, m):
        p = e_s[d, m].astype(f32) * inv[m]
        ds = (p * (dp_s[d, m] - delta[m])).astype(bf16)
        dk = dot(ds, q_s[m], 1, 0)
        dv = dot(p.astype(bf16), do_s[m], 1, 0)
        dqt_s[m] += dot(kv(d, 0, m), ds, 0, 0)
        return dk, dv

    def grad_home(d):
        return to_ctx(dkv.at[d - 1], gin.at[d - 1], b_send.at[d - 1], g_recv.at[d - 1], c - d)

    def grad_mate(d):
        k = reach - d
        return to_ctx(dkv.at[d - 1], rin.at[k - 1], b_send.at[d - 1], r_recv.at[k - 1], c + k)

    def grad_back():
        return to_ctx(zbuf, gin.at[reach - 1], b_send.at[reach - 1], g_recv.at[reach - 1],
                      c - reach)

    for d in range(reach - 1, 0, -1):
        @pl.when(c >= d)
        def _(d=d):
            for m in range(kv_count):
                dk, dv = second_pass(d, m)
                dkv[d - 1, 0, m] = dk.astype(bf16)
                dkv[d - 1, 1, m] = dv.astype(bf16)

            @pl.when(d <= s)
            def _():
                grad_home(d).start()

            @pl.when(d > s)
            def _():
                grad_mate(d).start()

    @pl.when(z > 0)
    def _():
        for m in range(kv_count):
            dk, dv = second_pass(reach, m)
            sum4[0, m] = dk
            sum4[1, m] = dv

    for m in range(kv_count):
        dk, dv = second_pass(0, m)
        own_grad[0, m] = dk
        own_grad[1, m] = dv

    def rs_copy(w, j):
        target = lax.rem(t + j, n_tp)
        return to_tp(part.at[w, target], rs_in.at[w, j - 1], rs_send.at[w, j - 1],
                     rs_recv.at[w, j - 1], target)

    def project(w, lhs, index, by_row):
        block = lhs[pl.ds(pl.multiple_of(index * local, local), local), :]

        def step(i, carry):
            cols = pl.ds(pl.multiple_of(i * tile, 128), tile)
            if by_row:
                part[w, index, :, cols] = dot(block, wo[:, cols], 1, 0).astype(bf16)
            else:
                part[w, index, :, cols] = dot(block, wqkv[cols, :], 1, 1).astype(bf16)
            return carry

        lax.fori_loop(0, width // tile, step, 0)

    for j in range(1, n_tp):
        project(0, att, lax.rem(t + j, n_tp), True)
        rs_copy(0, j).start()

    @pl.when(z > 0)
    def _():
        for k in range(1, reach):
            @pl.when(k <= s)
            def _(k=k):
                to_ctx(zbuf, rin.at[k - 1], b_send.at[k - 1], r_recv.at[k - 1], c).wait_recv()
                sum4[...] += rin[k - 1].astype(f32)
        zbuf[...] = sum4[...].astype(bf16)
        grad_back().start()

    for m in range(kv_count):
        for g in range(per_kv):
            h = m * per_kv + g
            grad = dqt_s[m, :, g * rows : (g + 1) * rows].T
            u = raw[:, h * head : (h + 1) * head]
            back[:, h * head : (h + 1) * head] = norm_rope_back(
                grad, u, qgain[...], cos_t[...], sin_t[...], half
            ).astype(bf16)

    project(0, att, t, True)

    def finish(w, base, dst):
        total = part[w, t].astype(f32)
        for j in range(1, n_tp):
            rs_copy(w, j).wait_recv()
            total += rs_in[w, j - 1].astype(f32)
        stage[w] = (base[t].astype(f32) + total).astype(bf16)
        copy = pltpu.make_async_copy(stage.at[w], dst, out_sem.at[w])
        copy.start()
        return copy

    written = [finish(0, xg, out_ref)]

    def gin_add(d):
        to_ctx(zbuf, gin.at[d - 1], b_send.at[d - 1], g_recv.at[d - 1], c).wait_recv()
        own_grad[...] += gin[d - 1].astype(f32)

    for d in range(1, reach):
        @pl.when(s + d < reach)
        def _(d=d):
            gin_add(d)

    @pl.when(z + 1 < nz)
    def _():
        gin_add(reach)

    for m in range(kv_count):
        k0 = qc + m * head
        u = raw[:, k0 : k0 + head]
        back[:, k0 : k0 + head] = norm_rope_back(
            own_grad[0, m], u, kgain[...], cos_t[...], sin_t[...], half
        ).astype(bf16)
        back[:, k0 + kc : k0 + kc + head] = own_grad[1, m].astype(bf16)

    for j in range(1, n_tp):
        project(1, back, lax.rem(t + j, n_tp), False)
        rs_copy(1, j).start()
    project(1, back, t, False)
    written.append(finish(1, gg, gout_ref))

    for w, copy in gathers:
        copy.wait_send()

    @pl.when(z + 1 < nz)
    def _():
        ahead().wait_send()

    for k in range(1, reach):
        @pl.when(s + k < reach)
        def _(k=k):
            own_to(k).wait_send()

        @pl.when((z > 0) & (k <= s))
        def _(k=k):
            relay_to(k).wait_send()

        @pl.when(c >= k)
        def _(k=k):
            grad_home(k).wait_send()

    @pl.when(z > 0)
    def _():
        grad_back().wait_send()

    for w in range(2):
        for j in range(1, n_tp):
            rs_copy(w, j).wait_send()
    for copy in written:
        copy.wait()


def on_device(
    tokens, result_grad, query_weight, key_weight, value_weight, output_weight, query_gain, key_gain
):
    n_ctx = lax.axis_size("ctx")
    n_tp = lax.axis_size("tp")
    local, width = tokens.shape
    rows = local * n_tp
    head = query_gain.shape[0]
    kv_count = key_weight.shape[1] // head
    per_kv = query_weight.shape[1] // key_weight.shape[1]
    reach = WINDOW // rows
    qc = kv_count * per_kv * head
    kc = kv_count * head
    qn = per_kv * rows
    tile = max(k for k in range(128, 1025, 128) if width % k == 0)
    exponent = jnp.arange(head // 2, dtype=f32) * (2.0 / head)
    frequency = jnp.power(f32(rope_theta), -exponent)
    frequency = jnp.concatenate([frequency, frequency])[None, :]
    any_spec = pl.BlockSpec(memory_space=pl.ANY)
    vmem_spec = pl.BlockSpec(memory_space=pltpu.VMEM)
    block = (2, kv_count, rows, head)
    dma = pltpu.SemaphoreType.DMA
    out = jax.ShapeDtypeStruct((local, width), bf16)
    return pl.pallas_call(
        functools.partial(kernel, n_ctx, n_tp, reach, per_kv, kv_count, head, tile),
        out_shape=(out, out),
        in_specs=[any_spec] * 6 + [vmem_spec] * 3,
        out_specs=(any_spec, any_spec),
        scratch_shapes=[
            pltpu.VMEM((width, qc + 2 * kc), bf16),
            pltpu.VMEM((qc, width), bf16),
            pltpu.VMEM((n_tp, local, width), bf16),
            pltpu.VMEM((n_tp, local, width), bf16),
            pltpu.VMEM((rows, qc + 2 * kc), f32),
            pltpu.VMEM((rows, head), f32),
            pltpu.VMEM((rows, head), f32),
            pltpu.VMEM((kv_count, qn, head), bf16),
            pltpu.VMEM((kv_count, qn, head), bf16),
            pltpu.VMEM((kv_count, head, qn), f32),
            pltpu.VMEM(block, bf16),
            pltpu.VMEM((reach,) + block, bf16),
            pltpu.VMEM((reach + 1, kv_count, rows, qn), bf16),
            pltpu.VMEM((reach + 1, kv_count, rows, qn), f32),
            pltpu.VMEM((kv_count, 1, qn), f32),
            pltpu.VMEM((kv_count, head, qn), f32),
            pltpu.VMEM((kv_count, head, qn), f32),
            pltpu.VMEM((rows, qc), bf16),
            pltpu.VMEM((reach - 1,) + block, bf16),
            pltpu.VMEM(block, f32),
            pltpu.VMEM(block, f32),
            pltpu.VMEM((reach,) + block, bf16),
            pltpu.VMEM((reach - 1,) + block, bf16),
            pltpu.VMEM(block, bf16),
            pltpu.VMEM((rows, qc + 2 * kc), bf16),
            pltpu.VMEM((2, n_tp, local, width), bf16),
            pltpu.VMEM((2, n_tp - 1, local, width), bf16),
            pltpu.VMEM((2, local, width), bf16),
            dma((6,)),
            dma((2, n_tp - 1)),
            dma((2, n_tp - 1)),
            dma((reach,)),
            dma((reach - 1,)),
            dma((reach,)),
            dma((reach,)),
            dma((reach,)),
            dma((reach - 1,)),
            dma((2, n_tp - 1)),
            dma((2, n_tp - 1)),
            dma((2,)),
        ],
        compiler_params=pltpu.CompilerParams(
            collective_id=0, has_side_effects=True, vmem_limit_bytes=60 * 1024 * 1024
        ),
    )(
        tokens, result_grad, query_weight, key_weight, value_weight, output_weight,
        query_gain[None, :], key_gain[None, :], frequency,
    )


def solution(mesh):
    in_specs = (
        P(("ctx", "tp"), None),
        P(("ctx", "tp"), None),
        P(None, "tp"),
        P(None, "tp"),
        P(None, "tp"),
        P("tp", None),
        P(),
        P(),
    )
    out_specs = (P(("ctx", "tp"), None), P(("ctx", "tp"), None))
    return jax.shard_map(
        on_device, mesh=mesh, in_specs=in_specs, out_specs=out_specs, check_vma=False
    )
```

time: 92.8 us -> 41.2 us (0.44); the launches traced: 91.3 us -> 41 us
  Pallas kernels: 0 us -> 36.9 us
  waiting for transfers between devices: 23.8 us -> 0 us
  starting transfers between devices: 21 us -> 0 us
  matrix products: 14 us -> 0 us
  between operations: 14.3 us -> 0.65 us
  other arithmetic: 12.8 us -> 0.6 us
  local copies, waits for them, and re-layouts: 5.53 us -> 2.91 us
    pallas_call x0 -> x1, Pallas kernels: none -> 36.9 us  [on_device(): pl.pallas_call(functools.partial(kernel, n_ctx, n_tp, reach, per_kv, kv_c...]
    ppermute x8 -> x0, starting transfers between devices: 20.8 us -> none  [from_behind(): return lax.ppermute(block, axis, route)]
    dot_general x14 -> x0, matrix products: 14 us -> none  [the longest x1 2.54 us: on_device(): jnp.einsum('nh,dh->nd', value_rows, value_weight, preferred_element_type=...]
    all_gather x1 -> x0, waiting for transfers between devices: 8.57 us -> none  [on_device(): portion = lax.all_gather(stacked, 'tp', axis=1, tiled=True)]
    reduce_scatter x2 -> x0, waiting for transfers between devices: 8.3 us -> none  [the longest x1 8.28 us: on_device(): lax.psum_scatter(summed.astype(jnp.bfloat16), 'tp', scatter_dimension=0,...]
    ppermute x8 -> x0, waiting for transfers between devices: 6.84 us -> none  [from_behind(): return lax.ppermute(block, axis, route)]
    convert_element_type x5 -> x0, other arithmetic: 5.24 us -> none  [the longest x1 2.1 us: on_device(): (result_grad.astype(jnp.float32) + grad_sum).astype(jnp.bfloat16)]
    another operation x5 -> x0, other arithmetic: 3.08 us -> none  [the longest x1 2.66 us: on_device(): stacked = jnp.stack([tokens, result_grad])]
  transfers between devices with their start and end apart: 11 -> 0, of which waited for: 5 -> 0; matrix products, arithmetic and copies ran while one was open for 15% -> 0% of each run, Pallas kernels for 0% -> 0%
where the time goes in v1:
time: 41.2 us; the launch traced here: 41 us
  Pallas kernels  36.9 us (90%)
  local copies, waits for them, and re-layouts  2.91 us (7%)
  between operations  0.65 us (2%)
  other arithmetic  0.6 us (1%)
    pallas_call x1, Pallas kernels, on_device(): pl.pallas_call(functools.partial(kernel, n_ctx, n_tp, reach, per_kv, kv_c...  36.9 us
    unnamed x4, local copies, waits for them, and re-layouts  2.91 us

profile of v1, /device:TPU:13, one launch (start us, length us, event | category | flops | bytes accessed | tf_op | source)
XLA Modules:
  0.0 41.0 jit_solution(16205523140324121153)
XLA Ops:
  0.6 0.6 %maximum_bitcast_fusion.freq = f32[1,128]{1,0:T(1,128)} fusion(f32[64]{0:T(128)S(1)} %negate_power_fusion), kind=kLoop, calls=%fused_computation | loop fusion | flops 128 | bytes 768 | tf_op jit(solution)/shard_map/broadcast_in_dim | solution.py:412
  1.2 36.9 %shard_map.95 = (bf16[128,2688]{1,0:T(8,128)(2,1)}, bf16[128,2688]{1,0:T(8,128)(2,1)}) custom-call(bf16[128,2688]{1,0:T(8,128)(2,1)} %tokens.1, bf16[128,2688]{1,0:T(8,128)(2,1)} %rgrad.1, bf16[2688,256]{1,0:T(8,128)(2,1)} %qw.1, bf16[2688,128]{1,0:T(8,128)(2,1)} %kw.1, bf16[2688,128]{1,0:T(8,128)(2,1)} %vw.1, bf16[256,2688]{1,0:T(8,128)(2,1)} %ow.1, ...), custom_call_target="tpu_custom_call" | custom-call | tf_op jit(solution)/shard_map/pallas_call | solution.py:418
  38.1 0.0 copy-start
  38.1 2.1 %copy.12 = bf16[128,2688]{1,0:T(8,128)(2,1)} copy(bf16[128,2688]{1,0:T(8,128)(2,1)} %get-tuple-element.4) | data formatting | bytes 1376256
  40.2 0.0 copy-done
  40.2 0.8 %copy.13 = bf16[128,2688]{1,0:T(8,128)(2,1)} copy(bf16[128,2688]{1,0:T(8,128)(2,1)S(1)} %copy-done) | data formatting | bytes 1376256
  (1 shorter events, 0.0 us)
Async XLA Ops:
  38.1 2.1 %copy-start = (bf16[128,2688]{1,0:T(8,128)(2,1)S(1)}, bf16[128,2688]{1,0:T(8,128)(2,1)}, u32[]{:S(2)}) copy-start(bf16[128,2688]{1,0:T(8,128)(2,1)} %get-tuple-element.5) | copy-start | bytes 2064388

commit v2 on v1

--- a/solution.py
+++ b/solution.py
@@ -63,11 +63,11 @@
         return pltpu.make_async_copy(src, dst, local_sem.at[i])
 
     loads = [
-        local_copy(0, tokens, xg.at[t]),
+        local_copy(0, tokens, xg.at[0]),
         local_copy(1, kw, wqkv.at[:, qc : qc + kc]),
         local_copy(2, vw, wqkv.at[:, qc + kc : qc + 2 * kc]),
         local_copy(3, qw, wqkv.at[:, :qc]),
-        local_copy(4, rgrad, gg.at[t]),
+        local_copy(4, rgrad, gg.at[0]),
         local_copy(5, ow, wo),
     ]
     for load in loads:
@@ -102,64 +102,101 @@
     def _():
         pl.semaphore_signal(barrier, inc=1, device_id={"ctx": c - reach}, device_id_type=MESH)
 
+    up = 2 * reach - 1 - 2 * s
+    down = 2 * s + 1
+    upper = (z + 1 < nz) & (up < reach)
+    lower = (z > 0) & (down < reach)
+
+    @pl.when(upper)
+    def _():
+        pl.semaphore_signal(barrier, inc=1, device_id={"ctx": c + up}, device_id_type=MESH)
+
+    @pl.when(lower)
+    def _():
+        pl.semaphore_signal(barrier, inc=1, device_id={"ctx": c - down}, device_id_type=MESH)
+
+    one, none = jnp.int32(1), jnp.int32(0)
     greeted = (
         n_tp - 1 + reach - 1
-        + jnp.where(z > 0, jnp.int32(1), jnp.int32(0))
-        + jnp.where(z + 1 < nz, jnp.int32(1), jnp.int32(0))
+        + jnp.where(z > 0, one, none)
+        + jnp.where(z + 1 < nz, one, none)
+        + jnp.where(upper, one, none)
+        + jnp.where(lower, one, none)
     )
-    pl.semaphore_wait(barrier, greeted)
-
-    gathers = []
-    for w, (src, dst) in enumerate(((tokens, xg), (rgrad, gg))):
-        for j in range(1, n_tp):
-            copy = to_tp(src, dst.at[t], ag_send.at[w, j - 1], ag_recv.at[w, j - 1],
-                         lax.rem(t + j, n_tp))
-            copy.start()
-            gathers.append((w, copy))
-
-    position = (c * rows + lax.broadcasted_iota(jnp.int32, (rows, head), 0)).astype(f32)
-    angles = position * freq[...]
+    def place(row):
+        return lax.rem(t + lax.div(row, local), n_tp) * local + lax.rem(row, local)
+
+    row = lax.broadcasted_iota(jnp.int32, (rows, head), 0)
+    angles = (c * rows + place(row)).astype(f32) * freq[...]
     lane = lax.broadcasted_iota(jnp.int32, (rows, head), 1)
     cos_t[...] = jnp.cos(angles)
     sines = jnp.sin(angles)
     sin_t[...] = jnp.where(lane < half, -sines, sines)
-
-    for i in (0, 1, 2):
-        loads[i].wait()
-    for w, copy in gathers:
+    pl.semaphore_wait(barrier, greeted)
+
+    gathers = []
+    for w, (src, dst) in enumerate(((tokens, xg), (rgrad, gg))):
+        for j in range(1, n_tp):
+            copy = to_tp(src, dst.at[n_tp - j], ag_send.at[w, j - 1], ag_recv.at[w, j - 1],
+                         lax.rem(t + j, n_tp))
+            copy.start()
+            gathers.append((w, copy))
+
+    spans = (slice(0, local), slice(local, rows))
+
+    def key_values(w, x):
+        span = spans[w]
+        raw[span, qc : qc + 2 * kc] = dot(x, wqkv[:, qc : qc + 2 * kc], 1, 0)
+        for m in range(kv_count):
+            u = raw[span, qc + m * head : qc + (m + 1) * head]
+            n = u * inverse_rms(u) * kgain[...]
+            kv_own[0, m, span] = rope(n, cos_t[span, :], sin_t[span, :], half).astype(bf16)
+            v0 = qc + kc + m * head
+            kv_own[1, m, span] = raw[span, v0 : v0 + head].astype(bf16)
+
+    def ahead(w):
+        return to_ctx(kv_own.at[:, :, spans[w]], halo.at[reach - 1, :, :, spans[w]],
+                      f_send.at[reach - 1, w], f_recv.at[reach - 1, w], c + reach)
+
+    def own_to(k, w):
+        return to_ctx(kv_own.at[:, :, spans[w]], halo.at[k - 1, :, :, spans[w]],
+                      f_send.at[k - 1, w], f_recv.at[k - 1, w], c + k)
+
+    def relay_to(k, w):
+        return to_ctx(halo.at[reach - 1, :, :, spans[w]],
+                      halo.at[reach - k - 1, :, :, spans[w]], f_relay.at[k - 1, w],
+                      f_recv.at[reach - k - 1, w], c - k)
+
+    def halo_wait(d, w):
+        own_span = kv_own.at[:, :, spans[w]]
+        to_ctx(own_span, halo.at[d - 1, :, :, spans[w]], f_send.at[d - 1, w],
+               f_recv.at[d - 1, w], c).wait_recv()
+
+    def sends_own(k):
+        return (s + k < reach) | (upper & (up == k))
+
+    def relays(k):
+        return (k <= s) & (2 * s - k != reach - 1)
+
+    for w in range(2):
         if w == 0:
-            copy.wait_recv()
-    x_all = xg[...].reshape(rows, width)
-    raw[:, qc : qc + 2 * kc] = dot(x_all, wqkv[:, qc : qc + 2 * kc], 1, 0)
-    for m in range(kv_count):
-        u = raw[:, qc + m * head : qc + (m + 1) * head]
-        n = u * inverse_rms(u) * kgain[...]
-        kv_own[0, m] = rope(n, cos_t[...], sin_t[...], half).astype(bf16)
-        v0 = qc + kc + m * head
-        kv_own[1, m] = raw[:, v0 : v0 + head].astype(bf16)
-
-    def ahead():
-        return to_ctx(kv_own, halo.at[reach - 1], f_send.at[reach - 1], f_recv.at[reach - 1],
-                      c + reach)
-
-    def own_to(k):
-        return to_ctx(kv_own, halo.at[k - 1], f_send.at[k - 1], f_recv.at[k - 1], c + k)
-
-    def relay_to(k):
-        return to_ctx(halo.at[reach - 1], halo.at[reach - k - 1], f_relay.at[k - 1],
-                      f_recv.at[reach - k - 1], c - k)
-
-    def halo_wait(d):
-        to_ctx(kv_own, halo.at[d - 1], f_send.at[d - 1], f_recv.at[d - 1], c).wait_recv()
-
-    @pl.when(z + 1 < nz)
-    def _():
-        ahead().start()
-
-    for k in range(1, reach):
-        @pl.when(s + k < reach)
-        def _(k=k):
-            own_to(k).start()
+            for i in (0, 1, 2):
+                loads[i].wait()
+            key_values(w, xg[0])
+        else:
+            for which, copy in gathers:
+                if which == 0:
+                    copy.wait_recv()
+            key_values(w, xg[1:].reshape(rows - local, width))
+
+        @pl.when(z + 1 < nz)
+        def _(w=w):
+            ahead(w).start()
+
+        for k in range(1, reach):
+            @pl.when(sends_own(k))
+            def _(k=k, w=w):
+                own_to(k, w).start()
 
     loads[3].wait()
     raw[:, :qc] = dot(xg[...].reshape(rows, width), wqkv[:, :qc], 1, 0)
@@ -188,8 +225,10 @@
             key, value = kv(d, 0, m), kv(d, 1, m)
             e = jnp.exp(dot(key, q_s[m], 1, 1) * score_scale)
             if d == 0 or d == reach:
-                key_row = lax.broadcasted_iota(jnp.int32, (rows, qn), 0)
-                query_row = lax.broadcasted_iota(jnp.int32, (rows, qn), 1) % rows
+                key_row = place(lax.broadcasted_iota(jnp.int32, (rows, 1), 0))
+                query_row = place(
+                    lax.rem(lax.broadcasted_iota(jnp.int32, (1, qn), 1), jnp.int32(rows))
+                )
                 keep = query_row >= key_row if d == 0 else query_row < key_row
                 e = jnp.where(keep, e, f32(0.0))
             total = jnp.sum(e, axis=0, keepdims=True)
@@ -208,17 +247,19 @@
 
     @pl.when(z > 0)
     def _():
-        halo_wait(reach)
-        for k in range(1, reach):
-            @pl.when(k <= s)
-            def _(k=k):
-                relay_to(k).start()
+        for w in range(2):
+            halo_wait(reach, w)
+            for k in range(1, reach):
+                @pl.when(relays(k))
+                def _(k=k, w=w):
+                    relay_to(k, w).start()
         first_pass(reach)
 
     for d in range(1, reach):
         @pl.when(c >= d)
         def _(d=d):
-            halo_wait(d)
+            halo_wait(d, 0)
+            halo_wait(d, 1)
             first_pass(d)
 
     inv, delta = [], []
@@ -240,16 +281,18 @@
         dqt_s[m] += dot(kv(d, 0, m), ds, 0, 0)
         return dk, dv
 
-    def grad_home(d):
-        return to_ctx(dkv.at[d - 1], gin.at[d - 1], b_send.at[d - 1], g_recv.at[d - 1], c - d)
-
-    def grad_mate(d):
+    def grad_home(d, w):
+        return to_ctx(dkv.at[d - 1, :, :, spans[w]], gin.at[d - 1, :, :, spans[w]],
+                      b_send.at[d - 1, w], g_recv.at[d - 1, w], c - d)
+
+    def grad_mate(d, w):
         k = reach - d
-        return to_ctx(dkv.at[d - 1], rin.at[k - 1], b_send.at[d - 1], r_recv.at[k - 1], c + k)
-
-    def grad_back():
-        return to_ctx(zbuf, gin.at[reach - 1], b_send.at[reach - 1], g_recv.at[reach - 1],
-                      c - reach)
+        return to_ctx(dkv.at[d - 1, :, :, spans[w]], rin.at[k - 1, :, :, spans[w]],
+                      b_send.at[d - 1, w], r_recv.at[k - 1, w], c + k)
+
+    def grad_back(w):
+        return to_ctx(zbuf.at[:, :, spans[w]], gin.at[reach - 1, :, :, spans[w]],
+                      b_send.at[reach - 1, w], g_recv.at[reach - 1, w], c - reach)
 
     for d in range(reach - 1, 0, -1):
         @pl.when(c >= d)
@@ -259,13 +302,14 @@
                 dkv[d - 1, 0, m] = dk.astype(bf16)
                 dkv[d - 1, 1, m] = dv.astype(bf16)
 
-            @pl.when(d <= s)
-            def _():
-                grad_home(d).start()
-
-            @pl.when(d > s)
-            def _():
-                grad_mate(d).start()
+            for w in (1, 0):
+                @pl.when((d <= s) | (d == down))
+                def _(w=w):
+                    grad_home(d, w).start()
+
+                @pl.when((d > s) & (d != down))
+                def _(w=w):
+                    grad_mate(d, w).start()
 
     @pl.when(z > 0)
     def _():
@@ -280,12 +324,11 @@
         own_grad[1, m] = dv
 
     def rs_copy(w, j):
-        target = lax.rem(t + j, n_tp)
-        return to_tp(part.at[w, target], rs_in.at[w, j - 1], rs_send.at[w, j - 1],
-                     rs_recv.at[w, j - 1], target)
+        return to_tp(part.at[w, j], rs_in.at[w, j - 1], rs_send.at[w, j - 1],
+                     rs_recv.at[w, j - 1], lax.rem(t + j, n_tp))
 
     def project(w, lhs, index, by_row):
-        block = lhs[pl.ds(pl.multiple_of(index * local, local), local), :]
+        block = lhs[index * local : (index + 1) * local, :]
 
         def step(i, carry):
             cols = pl.ds(pl.multiple_of(i * tile, 128), tile)
@@ -298,18 +341,21 @@
         lax.fori_loop(0, width // tile, step, 0)
 
     for j in range(1, n_tp):
-        project(0, att, lax.rem(t + j, n_tp), True)
+        project(0, att, j, True)
         rs_copy(0, j).start()
 
     @pl.when(z > 0)
     def _():
-        for k in range(1, reach):
-            @pl.when(k <= s)
-            def _(k=k):
-                to_ctx(zbuf, rin.at[k - 1], b_send.at[k - 1], r_recv.at[k - 1], c).wait_recv()
-                sum4[...] += rin[k - 1].astype(f32)
-        zbuf[...] = sum4[...].astype(bf16)
-        grad_back().start()
+        for w in (1, 0):
+            span = spans[w]
+            for k in range(1, reach):
+                @pl.when(relays(k))
+                def _(k=k, w=w, span=span):
+                    to_ctx(zbuf.at[:, :, span], rin.at[k - 1, :, :, span], b_send.at[k - 1, w],
+                           r_recv.at[k - 1, w], c).wait_recv()
+                    sum4[:, :, span] += rin[k - 1, :, :, span].astype(f32)
+            zbuf[:, :, span] = sum4[:, :, span].astype(bf16)
+            grad_back(w).start()
 
     for m in range(kv_count):
         for g in range(per_kv):
@@ -320,70 +366,77 @@
                 grad, u, qgain[...], cos_t[...], sin_t[...], half
             ).astype(bf16)
 
-    project(0, att, t, True)
+    project(0, att, 0, True)
 
     def finish(w, base, dst):
-        total = part[w, t].astype(f32)
+        total = part[w, 0].astype(f32)
         for j in range(1, n_tp):
             rs_copy(w, j).wait_recv()
             total += rs_in[w, j - 1].astype(f32)
-        stage[w] = (base[t].astype(f32) + total).astype(bf16)
+        stage[w] = (base[0].astype(f32) + total).astype(bf16)
         copy = pltpu.make_async_copy(stage.at[w], dst, out_sem.at[w])
         copy.start()
         return copy
 
     written = [finish(0, xg, out_ref)]
 
-    def gin_add(d):
-        to_ctx(zbuf, gin.at[d - 1], b_send.at[d - 1], g_recv.at[d - 1], c).wait_recv()
-        own_grad[...] += gin[d - 1].astype(f32)
-
-    for d in range(1, reach):
-        @pl.when(s + d < reach)
-        def _(d=d):
-            gin_add(d)
-
-    @pl.when(z + 1 < nz)
-    def _():
-        gin_add(reach)
-
-    for m in range(kv_count):
-        k0 = qc + m * head
-        u = raw[:, k0 : k0 + head]
-        back[:, k0 : k0 + head] = norm_rope_back(
-            own_grad[0, m], u, kgain[...], cos_t[...], sin_t[...], half
-        ).astype(bf16)
-        back[:, k0 + kc : k0 + kc + head] = own_grad[1, m].astype(bf16)
-
-    for j in range(1, n_tp):
-        project(1, back, lax.rem(t + j, n_tp), False)
-        rs_copy(1, j).start()
-    project(1, back, t, False)
+    def gin_add(d, w):
+        span = spans[w]
+        to_ctx(zbuf.at[:, :, span], gin.at[d - 1, :, :, span], b_send.at[d - 1, w],
+               g_recv.at[d - 1, w], c).wait_recv()
+        own_grad[:, :, span] += gin[d - 1, :, :, span].astype(f32)
+
+    for w in (1, 0):
+        span = spans[w]
+        for d in range(1, reach):
+            @pl.when(sends_own(d))
+            def _(d=d, w=w):
+                gin_add(d, w)
+
+        @pl.when(z + 1 < nz)
+        def _(w=w):
+            gin_add(reach, w)
+
+        for m in range(kv_count):
+            k0 = qc + m * head
+            u = raw[span, k0 : k0 + head]
+            back[span, k0 : k0 + head] = norm_rope_back(
+                own_grad[0, m, span], u, kgain[...], cos_t[span, :], sin_t[span, :], half
+            ).astype(bf16)
+            back[span, k0 + kc : k0 + kc + head] = own_grad[1, m, span].astype(bf16)
+
+        if w == 0:
+            project(1, back, 0, False)
+        else:
+            for j in range(1, n_tp):
+                project(1, back, j, False)
+                rs_copy(1, j).start()
     written.append(finish(1, gg, gout_ref))
 
     for w, copy in gathers:
         copy.wait_send()
 
-    @pl.when(z + 1 < nz)
-    def _():
-        ahead().wait_send()
-
-    for k in range(1, reach):
-        @pl.when(s + k < reach)
-        def _(k=k):
-            own_to(k).wait_send()
-
-        @pl.when((z > 0) & (k <= s))
-        def _(k=k):
-            relay_to(k).wait_send()
-
-        @pl.when(c >= k)
-        def _(k=k):
-            grad_home(k).wait_send()
-
-    @pl.when(z > 0)
-    def _():
-        grad_back().wait_send()
+    for w in range(2):
+        @pl.when(z + 1 < nz)
+        def _(w=w):
+            ahead(w).wait_send()
+
+        for k in range(1, reach):
+            @pl.when(sends_own(k))
+            def _(k=k, w=w):
+                own_to(k, w).wait_send()
+
+            @pl.when((z > 0) & relays(k))
+            def _(k=k, w=w):
+                relay_to(k, w).wait_send()
+
+            @pl.when(c >= k)
+            def _(k=k, w=w):
+                grad_home(k, w).wait_send()
+
+        @pl.when(z > 0)
+        def _(w=w):
+            grad_back(w).wait_send()
 
     for w in range(2):
         for j in range(1, n_tp):
@@ -452,12 +505,12 @@
             dma((6,)),
             dma((2, n_tp - 1)),
             dma((2, n_tp - 1)),
-            dma((reach,)),
-            dma((reach - 1,)),
-            dma((reach,)),
-            dma((reach,)),
-            dma((reach,)),
-            dma((reach - 1,)),
+            dma((reach, 2)),
+            dma((reach - 1, 2)),
+            dma((reach, 2)),
+            dma((reach, 2)),
+            dma((reach, 2)),
+            dma((reach - 1, 2)),
             dma((2, n_tp - 1)),
             dma((2, n_tp - 1)),
             dma((2,)),

time: 41.2 us -> 36.4 us (0.88)
  Pallas kernels: 36.9 us -> 32.1 us
    pallas_call x1, Pallas kernels: 36.9 us -> 32.1 us  [on_device(): pl.pallas_call(functools.partial(kernel, n_ctx, n_tp, reach, per_kv, kv_c...]
where the time goes in v2:
time: 36.4 us; the launch traced here: 36.3 us
  Pallas kernels  32.1 us (88%)
  local copies, waits for them, and re-layouts  2.91 us (8%)
  between operations  0.65 us (2%)
  other arithmetic  0.6 us (2%)
    pallas_call x1, Pallas kernels, on_device(): pl.pallas_call(functools.partial(kernel, n_ctx, n_tp, reach, per_kv, kv_c...  32.1 us
    unnamed x4, local copies, waits for them, and re-layouts  2.91 us

profile of v2, /device:TPU:13, one launch (start us, length us, event | category | flops | bytes accessed | tf_op | source)
XLA Modules:
  0.0 36.3 jit_solution(13347403322853773071)
XLA Ops:
  0.6 0.6 %maximum_bitcast_fusion.freq = f32[1,128]{1,0:T(1,128)} fusion(f32[64]{0:T(128)S(1)} %negate_power_fusion), kind=kLoop, calls=%fused_computation | loop fusion | flops 128 | bytes 768 | tf_op jit(solution)/shard_map/broadcast_in_dim | solution.py:465
  1.2 32.1 %shard_map.95 = (bf16[128,2688]{1,0:T(8,128)(2,1)}, bf16[128,2688]{1,0:T(8,128)(2,1)}) custom-call(bf16[128,2688]{1,0:T(8,128)(2,1)} %tokens.1, bf16[128,2688]{1,0:T(8,128)(2,1)} %rgrad.1, bf16[2688,256]{1,0:T(8,128)(2,1)} %qw.1, bf16[2688,128]{1,0:T(8,128)(2,1)} %kw.1, bf16[2688,128]{1,0:T(8,128)(2,1)} %vw.1, bf16[256,2688]{1,0:T(8,128)(2,1)} %ow.1, ...), custom_call_target="tpu_custom_call" | custom-call | tf_op jit(solution)/shard_map/pallas_call | solution.py:471
  33.3 0.0 copy-start
  33.3 2.1 %copy.12 = bf16[128,2688]{1,0:T(8,128)(2,1)} copy(bf16[128,2688]{1,0:T(8,128)(2,1)} %get-tuple-element.4) | data formatting | bytes 1376256
  35.4 0.0 copy-done
  35.4 0.8 %copy.13 = bf16[128,2688]{1,0:T(8,128)(2,1)} copy(bf16[128,2688]{1,0:T(8,128)(2,1)S(1)} %copy-done) | data formatting | bytes 1376256
  (1 shorter events, 0.0 us)
Async XLA Ops:
  33.3 2.1 %copy-start = (bf16[128,2688]{1,0:T(8,128)(2,1)S(1)}, bf16[128,2688]{1,0:T(8,128)(2,1)}, u32[]{:S(2)}) copy-start(bf16[128,2688]{1,0:T(8,128)(2,1)} %get-tuple-element.5) | copy-start | bytes 2064388

commit v3 on v2

--- a/solution.py
+++ b/solution.py
@@ -2,6 +2,7 @@
 
 import jax
 import jax.numpy as jnp
+import numpy as np
 from jax import lax
 from jax.experimental import pallas as pl
 from jax.experimental.pallas import tpu as pltpu
@@ -189,12 +190,17 @@
                     copy.wait_recv()
             key_values(w, xg[1:].reshape(rows - local, width))
 
+        for k in range(1, reach):
+            @pl.when(upper & (up == k))
+            def _(k=k, w=w):
+                own_to(k, w).start()
+
         @pl.when(z + 1 < nz)
         def _(w=w):
             ahead(w).start()
 
-        for k in range(1, reach):
-            @pl.when(sends_own(k))
+        for k in range(reach - 1, 0, -1):
+            @pl.when(s + k < reach)
             def _(k=k, w=w):
                 own_to(k, w).start()
 
@@ -460,9 +466,9 @@
     kc = kv_count * head
     qn = per_kv * rows
     tile = max(k for k in range(128, 1025, 128) if width % k == 0)
-    exponent = jnp.arange(head // 2, dtype=f32) * (2.0 / head)
-    frequency = jnp.power(f32(rope_theta), -exponent)
-    frequency = jnp.concatenate([frequency, frequency])[None, :]
+    exponent = np.arange(head // 2, dtype=np.float32) * np.float32(2.0 / head)
+    frequency = np.power(np.float32(rope_theta), -exponent)
+    frequency = jnp.asarray(np.concatenate([frequency, frequency])[None, :])
     any_spec = pl.BlockSpec(memory_space=pl.ANY)
     vmem_spec = pl.BlockSpec(memory_space=pltpu.VMEM)
     block = (2, kv_count, rows, head)

time: 36.4 us -> 35 us (0.962)
  Pallas kernels: 32.1 us -> 31.3 us
  other arithmetic: 0.6 us -> 0 us
    pallas_call x1, Pallas kernels: 32.1 us -> 31.3 us  [on_device(): pl.pallas_call(functools.partial(kernel, n_ctx, n_tp, reach, per_kv, kv_c...]
    broadcast_in_dim x1 -> x0, other arithmetic: 0.59 us -> none  [on_device(): frequency = jnp.concatenate([frequency, frequency])[None, :]]
where the time goes in v3:
time: 35 us; the launch traced here: 34.9 us
  Pallas kernels  31.3 us (89%)
  local copies, waits for them, and re-layouts  2.91 us (8%)
  between operations  0.65 us (2%)
    pallas_call x1, Pallas kernels, on_device(): pl.pallas_call(functools.partial(kernel, n_ctx, n_tp, reach, per_kv, kv_c...  31.3 us
    unnamed x4, local copies, waits for them, and re-layouts  2.91 us

profile of v3, /device:TPU:13, one launch (start us, length us, event | category | flops | bytes accessed | tf_op | source)
XLA Modules:
  0.0 34.9 jit_solution(9378714173469407244)
XLA Ops:
  0.6 31.3 %shard_map.104 = (bf16[128,2688]{1,0:T(8,128)(2,1)}, bf16[128,2688]{1,0:T(8,128)(2,1)}) custom-call(bf16[128,2688]{1,0:T(8,128)(2,1)} %tokens.1, bf16[128,2688]{1,0:T(8,128)(2,1)} %rgrad.1, bf16[2688,256]{1,0:T(8,128)(2,1)} %qw.1, bf16[2688,128]{1,0:T(8,128)(2,1)} %kw.1, bf16[2688,128]{1,0:T(8,128)(2,1)} %vw.1, bf16[256,2688]{1,0:T(8,128)(2,1)} %ow.1, ...), custom_call_target="tpu_custom_call" | custom-call | tf_op jit(solution)/shard_map/pallas_call | solution.py:477
  32.0 0.0 copy-start
  32.0 2.1 %copy.13 = bf16[128,2688]{1,0:T(8,128)(2,1)} copy(bf16[128,2688]{1,0:T(8,128)(2,1)} %get-tuple-element.4) | data formatting | bytes 1376256
  34.0 0.0 copy-done
  34.0 0.8 %copy.14 = bf16[128,2688]{1,0:T(8,128)(2,1)} copy(bf16[128,2688]{1,0:T(8,128)(2,1)S(1)} %copy-done) | data formatting | bytes 1376256
Async XLA Ops:
  32.0 2.1 %copy-start = (bf16[128,2688]{1,0:T(8,128)(2,1)S(1)}, bf16[128,2688]{1,0:T(8,128)(2,1)}, u32[]{:S(2)}) copy-start(bf16[128,2688]{1,0:T(8,128)(2,1)} %get-tuple-element.5) | copy-start | bytes 2064388
